TPU v7x, 256 devices: a whole 4x4x8 slice. The times are simulated.
256 devices in a mesh: row: 64 (over y, z, core), col: 4 (over x).
Axes of the slice: x: 4, y: 4, z: 8, core: 2. Of those that a mesh axis runs over, the one named last changes fastest.
Arguments:
- factor: float32 [8192, 8192], P('row', 'col'), may hold values from -0.125 to 0.125
- rhs: float32 [8192, 512], P('row', 'col'), may hold values from -6 to 6
- parent: int32 [7], replicated, may hold values from 4 to 6, as said below
- bounds: int32 [8], replicated, may hold values from 0 to 64, as said below
- slot: int32 [64], replicated, may hold values from 0 to 63, each once
- structure: int32 [7, 64], replicated, may hold values 0 or 1
Outputs:
- solution: float32 [8192, 512], P('row', 'col')
Inputs may be any that keep to these rules, and one draw needn't show every extreme that they name: parent[s] is 4 or 5 for s = 0 to 3, and 6 for s = 4, 5, 6 (the root is its own entry). bounds[0] = 0, bounds[7] = 64, strictly increasing; supernode s holds logical blocks bounds[s] to bounds[s+1] - 1. `slot`: a permutation.
All inputs are finite; a program needn't handle non-finite values.
Results may differ from a plain program's by a relative error of at most 0.0001.
Values sent between devices are 32-bit elements; how exact they have to be, the bound alone decides.
A program may use at most 64 MiB of HBM per device.

v0:
```python
import jax
import jax.numpy as jnp
from jax import lax
from jax.sharding import PartitionSpec as P

B = 128
RB = 1


def block_masks(parent, bounds, slot, structure):
    count = slot.shape[0]
    ar = jnp.arange(count, dtype=jnp.int32)
    logical = jnp.sum(jnp.where(slot[:, None] == ar[None, :], ar[:, None], 0), axis=0)
    node = jnp.sum((logical[:, None] >= bounds[None, 1:7]).astype(jnp.int32), axis=1)
    level = (node >= 4).astype(jnp.int32) + (node >= 6).astype(jnp.int32)
    nodes = jnp.arange(7, dtype=jnp.int32)
    grand = parent[parent]
    ancestor = ((nodes[None, :] == parent[:, None]) | (nodes[None, :] == grand[:, None])) & (
        nodes[None, :] != nodes[:, None]
    )
    node_hot = (node[:, None] == nodes[None, :]).astype(jnp.float32)
    perm_hot = (logical[:, None] == ar[None, :]).astype(jnp.float32)
    listed_store = jnp.dot(
        structure.astype(jnp.float32), perm_hot.T, precision=lax.Precision.HIGHEST
    )
    anc_pairs = jnp.dot(
        node_hot,
        jnp.dot(ancestor.astype(jnp.float32), node_hot.T, precision=lax.Precision.HIGHEST),
        precision=lax.Precision.HIGHEST,
    )
    list_pairs = jnp.dot(node_hot, listed_store, precision=lax.Precision.HIGHEST)
    link = (anc_pairs * list_pairs).T > 0.5
    same = node[:, None] == node[None, :]
    return (level, same, link)


def masked(block_rows, mask):
    rblocks, width = mask.shape
    bsz = block_rows.shape[0] // rblocks
    shaped = block_rows.reshape(rblocks, bsz, width, bsz) * mask[:, None, :, None].astype(
        jnp.float32
    )
    return shaped.reshape(block_rows.shape)


def body(factor, rhs, parent, bounds, slot, structure):
    level, same, link = block_masks(parent, bounds, slot, structure)
    first = lax.axis_index("row") * RB
    level_mine = lax.dynamic_slice_in_dim(level, first, RB, 0)
    same_mine = lax.dynamic_slice_in_dim(same, first, RB, 0)
    link_mine = lax.dynamic_slice_in_dim(link, first, RB, 0)
    full_rows = lax.all_gather(factor, "col", axis=1, tiled=True)
    diag_part = masked(full_rows, same_mine)
    link_part = masked(full_rows, link_mine)

    def product(matrix, vector):
        return jnp.dot(
            matrix,
            lax.all_gather(vector, "row", axis=0, tiled=True),
            precision=lax.Precision.HIGHEST,
            preferred_element_type=jnp.float32,
        )

    pieces = [rhs]
    accums = [jnp.zeros(p.shape, jnp.float32) for p in pieces]
    results = [jnp.zeros(p.shape, jnp.float32) for p in pieces]
    for section in range(3):
        rows = jnp.repeat(level_mine == section, B)[:, None]
        solved = jnp.where(rows, product(diag_part, pieces[0] - accums[0]), 0.0)
        results[0] = results[0] + solved
        if section < 2:
            accums[0] = accums[0] + product(link_part, solved)
    return results[0]


def solution(mesh):
    in_specs = (P("row", "col"), P("row", "col"), P(), P(), P(), P())
    out_specs = P("row", "col")
    return jax.shard_map(body, mesh=mesh, in_specs=in_specs, out_specs=out_specs, check_vma=False)
```

profile of v0, /device:TPU:1, one launch (start us, length us, event | category | flops | bytes accessed | tf_op | source)
XLA Modules:
  0.0 501.4 jit_solution(158808282834339269)
XLA Ops:
  6.5 0.7 all-gather.7.cloned.1.call-update
  7.3 0.7 all-gather.9.cloned.1.call-update
  8.1 0.7 slice.3
  8.8 0.7 select_reduce_fusion
  9.6 0.6 dynamic-slice
  10.2 0.7 dynamic_slice.9
  11.6 0.7 fusion.48
  12.3 51.4 %all-gather.7.cloned.1.call-done = f32[128,8192]{1,0:T(8,128)} async-done(((f32[128,2048]{1,0:T(8,128)}), f32[128,8192]{1,0:T(8,128)}) %all-gather.7.cloned.1.call-update) | async-done | bytes 4194320 | tf_op jit(solution)/shard_map/all_gather | solution.py:52
  63.8 82.7 %all-gather.9.cloned.1.call-done = f32[8192,128]{1,0:T(8,128)} async-done(((f32[128,128]{1,0:T(8,128)}), f32[8192,128]{1,0:T(8,128)}) %all-gather.9.cloned.1.call-update) | async-done | bytes 4194320 | tf_op jit(solution)/shard_map/all_gather | solution.py:59
  146.5 8.4 %fusion.15 = f32[128,128]{1,0:T(8,128)} fusion(f32[8192,128]{1,0:T(8,128)} %all-gather.9.cloned.1.call-done, f32[128,8192]{1,0:T(8,128)} %all-gather.7.cloned.1.call-done, f32[8192]{0:T(1024)S(1)} %broadcast_bitcast_fusion.1, pred[]{:T(512)} %bitcast), kind=kOutput, calls=%fused_computation.16 | convolution fusion | flops 1611677696 | bytes 8486913 | tf_op jit(solution)/shard_map/dot_general | solution.py:57
  155.0 0.6 gather_fusion
  155.6 0.2 fusion.35
  155.8 0.2 fusion.36
  156.0 0.3 fusion.33
  156.3 0.2 fusion.34
  156.7 74.7 %all-gather.11.cloned.1.call-done = f32[8192,128]{1,0:T(8,128)} async-done(((f32[128,128]{1,0:T(8,128)}), f32[8192,128]{1,0:T(8,128)}) %all-gather.11.cloned.1.call-update) | async-done | bytes 4194320 | tf_op jit(solution)/shard_map/all_gather | solution.py:59
  231.4 8.4 %fusion.50 = (f32[128,128]{1,0:T(8,128)}, f32[128,128]{1,0:T(8,128)S(1)}) fusion(f32[128,128]{1,0:T(8,128)S(1)} %copy-done.1, f32[8192,128]{1,0:T(8,128)} %all-gather.11.cloned.1.call-done, f32[128,8192]{1,0:T(8,128)} %all-gather.7.cloned.1.call-done, f32[8192]{0:T(1024)S(1)} %broadcast_bitcast_fusion), kind=kOutput, calls=%fused_computation.55 | convolution fusion | flops 1611677696 | bytes 8617984 | tf_op jit(solution)/shard_map/dot_general | solution.py:57
  239.8 0.2 all-gather.15.cloned.1.call-start
  240.7 75.6 %all-gather.13.cloned.1.call-done = f32[8192,128]{1,0:T(8,128)} async-done(((f32[128,128]{1,0:T(8,128)}), f32[8192,128]{1,0:T(8,128)}) %all-gather.13.cloned.1.call-update) | async-done | bytes 4194320 | tf_op jit(solution)/shard_map/all_gather | solution.py:59
  316.3 8.4 %fusion.18 = f32[128,128]{1,0:T(8,128)} fusion(f32[8192,128]{1,0:T(8,128)} %all-gather.13.cloned.1.call-done, f32[128,8192]{1,0:T(8,128)} %all-gather.7.cloned.1.call-done, f32[8192]{0:T(1024)S(1)} %broadcast_bitcast_fusion.1, pred[]{:T(512)} %bitcast.3), kind=kOutput, calls=%fused_computation.17 | convolution fusion | flops 1611677696 | bytes 8486913 | tf_op jit(solution)/shard_map/dot_general | solution.py:57
  324.8 76.4 %all-gather.15.cloned.1.call-done = f32[8192,128]{1,0:T(8,128)} async-done(((f32[128,128]{1,0:T(8,128)}), f32[8192,128]{1,0:T(8,128)}) %all-gather.15.cloned.1.call-update) | async-done | bytes 4194320 | tf_op jit(solution)/shard_map/all_gather | solution.py:59
  401.2 8.4 %fusion.30 = f32[128,128]{1,0:T(8,128)} fusion(f32[128,128]{1,0:T(8,128)S(1)} %copy-done.1, f32[128,128]{1,0:T(8,128)S(1)} %get-tuple-element.6, f32[8192,128]{1,0:T(8,128)} %all-gather.15.cloned.1.call-done, f32[128,8192]{1,0:T(8,128)} %all-gather.7.cloned.1.call-done, f32[8192]{0:T(1024)S(1)} %broadcast_bitcast_fusion), kind=kOutput, calls=%fused_computation.21 | convolution fusion | flops 1611694080 | bytes 8617984 | tf_op jit(solution)/shard_map/dot_general | solution.py:57
  410.3 75.8 %all-gather.17.cloned.1.call-done = f32[8192,128]{1,0:T(8,128)} async-done(((f32[128,128]{1,0:T(8,128)}), f32[8192,128]{1,0:T(8,128)}) %all-gather.17.cloned.1.call-update) | async-done | bytes 4194320 | tf_op jit(solution)/shard_map/all_gather | solution.py:59
  486.1 8.4 %fusion.24 = f32[128,128]{1,0:T(8,128)} fusion(f32[8192,128]{1,0:T(8,128)} %all-gather.17.cloned.1.call-done, f32[128,8192]{1,0:T(8,128)} %all-gather.7.cloned.1.call-done, f32[8192]{0:T(1024)S(1)} %broadcast_bitcast_fusion.1, f32[128,128]{1,0:T(8,128)S(1)} %copy-done.2, f32[128,128]{1,0:T(8,128)S(1)} %copy-done.3, pred[]{:T(512)} %bitcast.6), kind=kOutput, calls=%fused_computation.19 | convolution fusion | flops 1611710464 | bytes 8617985 | tf_op jit(solution)/shard_map/dot_general | solution.py:57
  (26 shorter events, 0.5 us)
Async XLA Ops:
  6.5 57.2 %all-gather.7.cloned.1.call-start = ((), (), s32[]{:S(2)}) async-start(), calls=%async_computation | async-start | bytes 5242880 | tf_op jit(solution)/shard_map/all_gather | solution.py:52
  7.3 139.2 %all-gather.9.cloned.1.call-start = ((), (), s32[]{:S(2)}) async-start(), calls=%async_computation.1 | async-start | bytes 4259840 | tf_op jit(solution)/shard_map/all_gather | solution.py:59
  8.0 223.4 %all-gather.11.cloned.1.call-start = ((), (), s32[]{:S(2)}) async-start(), calls=%async_computation.2 | async-start | bytes 4259840 | tf_op jit(solution)/shard_map/all_gather | solution.py:59
  146.5 8.5 %copy-start = (s32[7]{0:T(128)S(1)}, s32[7]{0:T(128)}, u32[]{:S(2)}) copy-start(s32[7]{0:T(128)} %param.8) | copy-start | bytes 88
  146.5 9.4 %copy-start.4 = (s32[7,64]{1,0:T(8,128)S(1)}, s32[7,64]{1,0:T(8,128)}, u32[]{:S(2)}) copy-start(s32[7,64]{1,0:T(8,128)} %param.11) | copy-start | bytes 5380
  146.5 84.9 %copy-start.1 = (f32[128,128]{1,0:T(8,128)S(1)}, f32[128,128]{1,0:T(8,128)}, u32[]{:S(2)}) copy-start(f32[128,128]{1,0:T(8,128)} %param.7) | copy-start | bytes 196612
  154.9 161.4 %all-gather.13.cloned.1.call-start = ((), (), s32[]{:S(2)}) async-start(), calls=%async_computation.3 | async-start | bytes 4259840 | tf_op jit(solution)/shard_map/all_gather | solution.py:59
  239.8 161.4 %all-gather.15.cloned.1.call-start = ((), (), s32[]{:S(2)}) async-start(), calls=%async_computation.4 | async-start | bytes 4259840 | tf_op jit(solution)/shard_map/all_gather | solution.py:59
  324.7 161.4 %all-gather.17.cloned.1.call-start = ((), (), s32[]{:S(2)}) async-start(), calls=%async_computation.5 | async-start | bytes 4259840 | tf_op jit(solution)/shard_map/all_gather | solution.py:59
  401.2 84.9 %copy-start.2 = (f32[128,128]{1,0:T(8,128)S(1)}, f32[128,128]{1,0:T(8,128)}, u32[]{:S(2)}) copy-start(f32[128,128]{1,0:T(8,128)} %fusion.15) | copy-start | bytes 196612
  401.2 84.9 %copy-start.3 = (f32[128,128]{1,0:T(8,128)S(1)}, f32[128,128]{1,0:T(8,128)}, u32[]{:S(2)}) copy-start(f32[128,128]{1,0:T(8,128)} %fusion.18) | copy-start | bytes 196612
Sparse Core Ops, SparseCore 0:
  9.2 54.5 all-gather.6
  66.5 79.8 all-gather.8
  155.0 76.3 all-gather.10
  239.9 76.3 all-gather.12
  324.8 76.3 all-gather.14
  409.8 76.3 all-gather.16
where the time goes:
time: 501 us
  waiting for transfers between devices  438 us (87%)
  matrix products  42.9 us (9%)
  between operations  15.6 us (3%)
    all_gather x5, waiting for transfers between devices, product(): lax.all_gather(vector, 'row', axis=0, tiled=True)  385 us
    all_gather x1, waiting for transfers between devices, body(): full_rows = lax.all_gather(factor, 'col', axis=1, tiled=True)  51.4 us
    dot_general x5, matrix products, product(): jnp.dot(matrix, lax.all_gather(vector, 'row', axis=0, tiled=True), precis...  42 us
  transfers between devices with their start and end apart: 6, of which 6 were waited for; matrix products, arithmetic and copies ran while one was open for 1% of the time, Pallas kernels for 0%

commit v1 on v0

--- a/solution.py
+++ b/solution.py
@@ -56,7 +56,9 @@
     def product(matrix, vector):
         return jnp.dot(
             matrix,
-            lax.all_gather(vector, "row", axis=0, tiled=True),
+            jnp.concatenate(
+                lax.all_to_all(jnp.stack([vector] * lax.axis_size("row")), "row", 0, 0), axis=0
+            ),
             precision=lax.Precision.HIGHEST,
             preferred_element_type=jnp.float32,
         )

time: 501 us -> 578 us (1.15)
  blocking collectives: 0 us -> 102 us
  waiting for transfers between devices: 438 us -> 378 us
  starting transfers between devices: 0.38 us -> 31.5 us
  local copies, waits for them, and re-layouts: 2.79 us -> 13.3 us
  matrix products: 42.9 us -> 37 us
    all_gather x5 -> x0, waiting for transfers between devices: 385 us -> none  [product(): lax.all_gather(vector, 'row', axis=0, tiled=True)]
    all_to_all x0 -> x4, waiting for transfers between devices: none -> 326 us  [product(): lax.all_to_all(jnp.stack([vector] * lax.axis_size('row')), 'row', 0, 0)]
    all_to_all x0 -> x1, blocking collectives: none -> 102 us  [product(): lax.all_to_all(jnp.stack([vector] * lax.axis_size('row')), 'row', 0, 0)]
    all_to_all x0 -> x4, starting transfers between devices: none -> 31.5 us  [product(): lax.all_to_all(jnp.stack([vector] * lax.axis_size('row')), 'row', 0, 0)]
    another operation x0 -> x5, local copies, waits for them, and re-layouts: none -> 11.2 us  [product(): jnp.stack([vector] * lax.axis_size('row'))]
    dot_general x5, matrix products: 42 us -> 36.1 us  [product(): jnp.dot(matrix, jnp.concatenate(lax.all_to_all(jnp.stack([vector] * lax.a...]
  transfers between devices with their start and end apart: 6 -> 5, of which waited for: 6 -> 5; matrix products, arithmetic and copies ran while one was open for 1% -> 1% of each run, Pallas kernels for 0% -> 0%
where the time goes in v1:
time: 578 us
  waiting for transfers between devices  378 us (65%)
  blocking collectives  102 us (18%)
  matrix products  37 us (6%)
  starting transfers between devices  31.5 us (5%)
  between operations  15.4 us (3%)
  local copies, waits for them, and re-layouts  13.3 us (2%)
    all_to_all x4, waiting for transfers between devices, product(): lax.all_to_all(jnp.stack([vector] * lax.axis_size('row')), 'row', 0, 0)  326 us
    all_to_all x1, blocking collectives, product(): lax.all_to_all(jnp.stack([vector] * lax.axis_size('row')), 'row', 0, 0)  102 us
    all_gather x1, waiting for transfers between devices, body(): full_rows = lax.all_gather(factor, 'col', axis=1, tiled=True)  50.8 us
    dot_general x5, matrix products, product(): jnp.dot(matrix, jnp.concatenate(lax.all_to_all(jnp.stack([vector] * lax.a...  36.1 us
    all_to_all x4, starting transfers between devices, product(): lax.all_to_all(jnp.stack([vector] * lax.axis_size('row')), 'row', 0, 0)  31.5 us
  transfers between devices with their start and end apart: 5, of which 5 were waited for; matrix products, arithmetic and copies ran while one was open for 1% of the time, Pallas kernels for 0%

profile of v1, /device:TPU:1, one launch (start us, length us, event | category | flops | bytes accessed | tf_op | source)
XLA Modules:
  0.0 577.8 jit_solution(10657999921167004660)
XLA Ops:
  6.5 3.3 stack.10
  9.8 13.5 %all-to-all-start = ((f32[64,128,128]{2,1,0:T(8,128)}), f32[64,128,128]{2,1,0:T(8,128)}, u32[]{:S(2)}, u32[]{:S(2)}) async-start(f32[64,128,128]{2,1,0:T(8,128)} %stack.10), calls=%async_computation | async-start | bytes 8388608 | tf_op jit(solution)/shard_map/all_to_all | solution.py:60
  23.4 0.7 all-gather.2.cloned.1.call-update
  24.3 0.6 dynamic-slice
  24.9 0.6 dynamic_slice.9
  26.2 0.7 fusion.48
  26.9 50.8 %all-gather.2.cloned.1.call-done = f32[128,8192]{1,0:T(8,128)} async-done(((f32[128,2048]{1,0:T(8,128)}), f32[128,8192]{1,0:T(8,128)}) %all-gather.2.cloned.1.call-update) | async-done | bytes 4194320 | tf_op jit(solution)/shard_map/all_gather | solution.py:52
  77.7 41.5 %all-to-all-done = f32[64,128,128]{2,1,0:T(8,128)} async-done(((f32[64,128,128]{2,1,0:T(8,128)}), f32[64,128,128]{2,1,0:T(8,128)}, u32[]{:S(2)}, u32[]{:S(2)}) %all-to-all-start) | async-done | bytes 4194336 | tf_op jit(solution)/shard_map/all_to_all | solution.py:60
  119.2 7.8 %fusion.15 = f32[128,128]{1,0:T(8,128)S(1)} fusion(f32[8192,128]{1,0:T(8,128)} %bitcast.3, f32[128,8192]{1,0:T(8,128)} %all-gather.2.cloned.1.call-done, f32[8192]{0:T(1024)S(1)} %broadcast_bitcast_fusion.1, pred[]{:T(512)} %bitcast), kind=kOutput, calls=%fused_computation.16 | convolution fusion | flops 1611677696 | bytes 8486913 | tf_op jit(solution)/shard_map/dot_general | solution.py:57
  127.0 2.5 stack.11
  129.5 6.1 %all-to-all-start.1 = ((f32[64,128,128]{2,1,0:T(8,128)}), f32[64,128,128]{2,1,0:T(8,128)}, u32[]{:S(2)}, u32[]{:S(2)}) async-start(f32[64,128,128]{2,1,0:T(8,128)} %stack.11), calls=%async_computation.1 | async-start | bytes 8388608 | tf_op jit(solution)/shard_map/all_to_all | solution.py:60
  135.6 0.6 gather_fusion
  137.3 94.2 %all-to-all-done.1 = f32[64,128,128]{2,1,0:T(8,128)} async-done(((f32[64,128,128]{2,1,0:T(8,128)}), f32[64,128,128]{2,1,0:T(8,128)}, u32[]{:S(2)}, u32[]{:S(2)}) %all-to-all-start.1) | async-done | bytes 4194336 | tf_op jit(solution)/shard_map/all_to_all | solution.py:60
  231.5 7.8 %fusion.50 = (f32[128,128]{1,0:T(8,128)S(1)}, f32[128,128]{1,0:T(8,128)S(1)}) fusion(f32[128,128]{1,0:T(8,128)S(1)} %copy-done.2, f32[8192,128]{1,0:T(8,128)} %bitcast.7, f32[128,8192]{1,0:T(8,128)} %all-gather.2.cloned.1.call-done, f32[8192]{0:T(1024)S(1)} %broadcast_bitcast_fusion), kind=kOutput, calls=%fused_computation.55 | convolution fusion | flops 1611677696 | bytes 8617984 | tf_op jit(solution)/shard_map/dot_general | solution.py:57
  239.3 2.5 stack.12
  241.7 5.9 %all-to-all-start.2 = ((f32[64,128,128]{2,1,0:T(8,128)}), f32[64,128,128]{2,1,0:T(8,128)}, u32[]{:S(2)}, u32[]{:S(2)}) async-start(f32[64,128,128]{2,1,0:T(8,128)} %stack.12), calls=%async_computation.2 | async-start | bytes 8388608 | tf_op jit(solution)/shard_map/all_to_all | solution.py:60
  248.3 95.3 %all-to-all-done.2 = f32[64,128,128]{2,1,0:T(8,128)} async-done(((f32[64,128,128]{2,1,0:T(8,128)}), f32[64,128,128]{2,1,0:T(8,128)}, u32[]{:S(2)}, u32[]{:S(2)}) %all-to-all-start.2) | async-done | bytes 4194336 | tf_op jit(solution)/shard_map/all_to_all | solution.py:60
  343.5 7.8 %fusion.18 = f32[128,128]{1,0:T(8,128)S(1)} fusion(f32[8192,128]{1,0:T(8,128)} %bitcast.8, f32[128,8192]{1,0:T(8,128)} %all-gather.2.cloned.1.call-done, f32[8192]{0:T(1024)S(1)} %broadcast_bitcast_fusion.1, pred[]{:T(512)} %bitcast.4), kind=kOutput, calls=%fused_computation.17 | convolution fusion | flops 1611677696 | bytes 8486913 | tf_op jit(solution)/shard_map/dot_general | solution.py:57
  351.9 102.0 %all_to_all.25 = f32[64,128,128]{2,1,0:T(8,128)S(1)} all-to-all(f32[64,128,128]{2,1,0:T(8,128)S(1)} %stack.13), channel_id=1, replica_groups=mesh['row'=64,'col'=4] {'row'}, dimensions={0} | all-to-all | bytes 8388608 | tf_op jit(solution)/shard_map/all_to_all | solution.py:60
  453.9 4.3 fusion.30
  458.2 2.5 stack.14
  460.7 6.0 %all-to-all-start.4 = ((f32[64,128,128]{2,1,0:T(8,128)}), f32[64,128,128]{2,1,0:T(8,128)}, u32[]{:S(2)}, u32[]{:S(2)}) async-start(f32[64,128,128]{2,1,0:T(8,128)} %stack.14), calls=%async_computation.4 | async-start | bytes 8388608 | tf_op jit(solution)/shard_map/all_to_all | solution.py:60
  467.3 95.3 %all-to-all-done.4 = f32[64,128,128]{2,1,0:T(8,128)} async-done(((f32[64,128,128]{2,1,0:T(8,128)}), f32[64,128,128]{2,1,0:T(8,128)}, u32[]{:S(2)}, u32[]{:S(2)}) %all-to-all-start.4) | async-done | bytes 4194336 | tf_op jit(solution)/shard_map/all_to_all | solution.py:60
  562.6 8.4 %fusion.24 = f32[128,128]{1,0:T(8,128)} fusion(f32[8192,128]{1,0:T(8,128)} %bitcast.11, f32[128,8192]{1,0:T(8,128)} %all-gather.2.cloned.1.call-done, f32[8192]{0:T(1024)S(1)} %broadcast_bitcast_fusion.1, f32[128,128]{1,0:T(8,128)S(1)} %fusion.15, f32[128,128]{1,0:T(8,128)S(1)} %fusion.18, pred[]{:T(512)} %bitcast.9), kind=kOutput, calls=%fused_computation.19 | convolution fusion | flops 1611710464 | bytes 8617985 | tf_op jit(solution)/shard_map/dot_general | solution.py:57
  (27 shorter events, 1.9 us)
Async XLA Ops:
  9.8 14.2 %copy-start.4 = (s32[8]{0:T(128)S(1)}, s32[8]{0:T(128)}, u32[]{:S(2)}) copy-start(s32[8]{0:T(128)} %param.9) | copy-start | bytes 100
  9.8 14.3 %copy-start.5 = (s32[64]{0:T(128)S(1)}, s32[64]{0:T(128)}, u32[]{:S(2)}) copy-start(s32[64]{0:T(128)} %param.10) | copy-start | bytes 772
  9.8 109.4 %all-to-all-start = ((f32[64,128,128]{2,1,0:T(8,128)}), f32[64,128,128]{2,1,0:T(8,128)}, u32[]{:S(2)}, u32[]{:S(2)}) async-start(f32[64,128,128]{2,1,0:T(8,128)} %stack.10), calls=%async_computation | async-start | bytes 8388608 | tf_op jit(solution)/shard_map/all_to_all | solution.py:60
  23.3 54.4 %all-gather.2.cloned.1.call-start = ((), (), s32[]{:S(2)}) async-start(), calls=%async_computation.5 | async-start | bytes 5242880 | tf_op jit(solution)/shard_map/all_gather | solution.py:52
  129.5 6.1 %copy-start = (s32[7]{0:T(128)S(1)}, s32[7]{0:T(128)}, u32[]{:S(2)}) copy-start(s32[7]{0:T(128)} %param.8) | copy-start | bytes 88
  129.5 7.0 %copy-start.3 = (s32[7,64]{1,0:T(8,128)S(1)}, s32[7,64]{1,0:T(8,128)}, u32[]{:S(2)}) copy-start(s32[7,64]{1,0:T(8,128)} %param.11) | copy-start | bytes 5380
  129.5 102.0 %copy-start.2 = (f32[128,128]{1,0:T(8,128)S(1)}, f32[128,128]{1,0:T(8,128)}, u32[]{:S(2)}) copy-start(f32[128,128]{1,0:T(8,128)} %param.7) | copy-start | bytes 196612
  129.5 102.0 %all-to-all-start.1 = ((f32[64,128,128]{2,1,0:T(8,128)}), f32[64,128,128]{2,1,0:T(8,128)}, u32[]{:S(2)}, u32[]{:S(2)}) async-start(f32[64,128,128]{2,1,0:T(8,128)} %stack.11), calls=%async_computation.1 | async-start | bytes 8388608 | tf_op jit(solution)/shard_map/all_to_all | solution.py:60
  241.7 101.8 %all-to-all-start.2 = ((f32[64,128,128]{2,1,0:T(8,128)}), f32[64,128,128]{2,1,0:T(8,128)}, u32[]{:S(2)}, u32[]{:S(2)}) async-start(f32[64,128,128]{2,1,0:T(8,128)} %stack.12), calls=%async_computation.2 | async-start | bytes 8388608 | tf_op jit(solution)/shard_map/all_to_all | solution.py:60
  351.9 102.0 %copy-start.1 = (f32[128,8192]{1,0:T(8,128)S(1)}, f32[128,8192]{1,0:T(8,128)}, u32[]{:S(2)}) copy-start(f32[128,8192]{1,0:T(8,128)} %all-gather.2.cloned.1.call-done) | copy-start | bytes 12582916
  460.7 101.9 %all-to-all-start.4 = ((f32[64,128,128]{2,1,0:T(8,128)}), f32[64,128,128]{2,1,0:T(8,128)}, u32[]{:S(2)}, u32[]{:S(2)}) async-start(f32[64,128,128]{2,1,0:T(8,128)} %stack.14), calls=%async_computation.4 | async-start | bytes 8388608 | tf_op jit(solution)/shard_map/all_to_all | solution.py:60
Sparse Core Ops, SparseCore 0:
  26.0 51.7 all-gather.1
